TPU v7x, 128 devices: a whole 4x4x4 slice. The times are simulated.
128 devices in a mesh: gz: 8 (over x, core), xy: 16 (over y, z).
Axes of the slice: x: 4, y: 4, z: 4, core: 2. Of those that a mesh axis runs over, the one named last changes fastest.
Arguments:
- parent_feat: bfloat16 [128, 64, 2048], P(('gz', 'xy')), may hold values from -6 to 6
- parent_cell: int32 [128, 2048], P(('gz', 'xy')), may hold values from 0 to 255
- send_count: int32 [128, 128], P(('gz', 'xy')), may hold values from 1 to 16, as said below
- up_weight: bfloat16 [8, 64, 64], replicated, may hold values from -0.75 to 0.75
- conv_one: bfloat16 [27, 64, 64], replicated, may hold values from -0.15625 to 0.15625
- conv_two: bfloat16 [27, 64, 64], replicated, may hold values from -0.15625 to 0.15625
- child_mask: int32 [32, 8, 1024], P('xy', None, 'gz'), may hold values 0 or 1
- cotangent: bfloat16 [64, 32, 8, 1024], P(None, 'xy', None, 'gz'), may hold values from -6 to 6
Outputs:
- decoded: bfloat16 [64, 32, 8, 1024], P(None, 'xy', None, 'gz')
- grad_parent: bfloat16 [128, 64, 2048], P(('gz', 'xy'))
- grad_one: float32 [27, 64, 64], replicated
- grad_two: float32 [27, 64, 64], replicated
- grad_up: float32 [8, 64, 64], replicated
Inputs may be any that keep to these rules, and one draw needn't show every extreme that they name: `send_count`: some receiver gets 16 live slots from every sender, and every sender fills all 16 slots to some receiver. `parent_cell`: several slots may name the same parent voxel; their features add.
All inputs are finite; a program needn't handle non-finite values. No bound on the sum of `child_mask` on one device may be relied on, other than what follows from the above.
Results may differ from a plain program's by a relative error of at most 0.008.
Values may be sent and summed in bfloat16 or wider, within the bound.
No kernel may reach another device: no remote copies, remote signals or barrier semaphores. Data moves between devices by JAX's collectives and lax.ppermute only.
A program may use at most 64 MiB of HBM per device.

v0:
```python
import math
import jax
import jax.numpy as jnp
from jax import lax
from jax.sharding import PartitionSpec as P

OFFSETS = [(a, b, c) for a in (-1, 0, 1) for b in (-1, 0, 1) for c in (-1, 0, 1)]


def with_halo(shard, sides, width):
    for axis, dim in sides:
        devices, length = (lax.axis_size(axis), shard.shape[dim])
        up = [(i, (i + 1) % devices) for i in range(devices - 1)]
        down = [(j, i) for i, j in up]
        last = lax.slice_in_dim(shard, length - width, length, axis=dim)
        first = lax.slice_in_dim(shard, 0, width, axis=dim)
        before = lax.ppermute(last, axis, up)
        after = lax.ppermute(first, axis, down)
        shard = jnp.concatenate([before, shard, after], axis=dim)
    return shard


def extend(field):
    bordered = with_halo(field, (("xy", 1), ("gz", 3)), 1)
    return jnp.pad(bordered, ((0, 0), (0, 0), (1, 1), (0, 0)))


def window(padded, offset, direction, shape):
    nx, ny, nz = (shape[1], shape[2], shape[3])
    ox, oy, oz = (offset[0] * direction, offset[1] * direction, offset[2] * direction)
    part = padded[:, 1 + ox : 1 + ox + nx, 1 + oy : 1 + oy + ny, 1 + oz : 1 + oz + nz]
    return part.reshape(shape[0], -1)


def orient(matrix, direction):
    return matrix if direction > 0 else matrix.T


def convolve(padded, weights, direction, shape):
    total = jnp.zeros((shape[0], shape[1] * shape[2] * shape[3]), jnp.float32)
    for index, offset in enumerate(OFFSETS):
        total = total + jnp.dot(
            orient(weights[index], direction),
            window(padded, offset, direction, shape),
            preferred_element_type=jnp.float32,
        )
    return total.reshape(shape)


def weight_terms(delta, padded, shape):
    flat = delta.reshape(shape[0], -1)
    terms = [
        lax.dot_general(
            flat,
            window(padded, offset, 1, shape),
            (((1,), (1,)), ((), ())),
            preferred_element_type=jnp.float32,
        )
        for offset in OFFSETS
    ]
    return jnp.stack(terms)


def silu_slope(value):
    sig = jax.nn.sigmoid(value)
    return sig * (1.0 + value * (1.0 - sig))


def local(
    parent_feat, parent_cell, send_count, up_weight, conv_one, conv_two, child_mask, cotangent
):
    channels, size_x, size_y, size_z = cotangent.shape
    shape = cotangent.shape
    count_gz = lax.axis_size("gz")
    count_xy = lax.axis_size("xy")
    devices_all = count_gz * count_xy
    slot_total = parent_feat.shape[2]
    capacity = slot_total // devices_all
    half_x, half_y, half_z = (size_x // 2, size_y // 2, size_z // 2)
    parent_total = half_x * half_y * half_z
    slot_pos = jnp.arange(slot_total, dtype=jnp.int32) % capacity
    live = slot_pos < jnp.repeat(send_count[0], capacity)
    feats = jnp.where(live[None, :], parent_feat[0], jnp.zeros_like(parent_feat[0]))
    got_feat, got_cell = (
        lax.all_to_all(feats, ("gz", "xy"), split_axis=1, concat_axis=1, tiled=True),
        lax.all_to_all(parent_cell, ("gz", "xy"), split_axis=1, concat_axis=1, tiled=True),
    )
    got_cell = got_cell.reshape(slot_total)
    onehot = (got_cell[:, None] == jnp.arange(parent_total, dtype=jnp.int32)[None, :]).astype(
        jnp.bfloat16
    )
    parent_grid = jnp.dot(got_feat, onehot, preferred_element_type=jnp.float32).astype(jnp.bfloat16)
    up8 = jnp.einsum("ocd,dq->ocq", up_weight, parent_grid, preferred_element_type=jnp.float32)
    up = (
        up8.reshape(2, 2, 2, channels, half_x, half_y, half_z)
        .transpose(3, 4, 0, 5, 1, 6, 2)
        .reshape(shape)
    )
    maskf = child_mask.astype(jnp.float32)
    lifted = (maskf * up).astype(jnp.bfloat16)
    lifted_pad = extend(lifted)
    first_pre = convolve(lifted_pad, conv_one, 1, shape)
    first_act = (maskf * jax.nn.silu(first_pre)).astype(jnp.bfloat16)
    first_pad = extend(first_act)
    second_pre = convolve(first_pad, conv_two, 1, shape)
    decoded = (maskf * jax.nn.silu(second_pre)).astype(jnp.bfloat16)
    delta_two = (cotangent.astype(jnp.float32) * maskf * silu_slope(second_pre)).astype(
        jnp.bfloat16
    )
    term_two = weight_terms(delta_two, first_pad, shape)
    back_one = convolve(extend(delta_two), conv_two, -1, shape)
    delta_one = (back_one * maskf * silu_slope(first_pre)).astype(jnp.bfloat16)
    term_one = weight_terms(delta_one, lifted_pad, shape)
    delta_up = (convolve(extend(delta_one), conv_one, -1, shape) * maskf).astype(jnp.bfloat16)
    du8 = (
        delta_up.reshape(channels, half_x, 2, half_y, 2, half_z, 2)
        .transpose(2, 4, 6, 0, 1, 3, 5)
        .reshape(8, channels, parent_total)
    )
    term_up = jnp.einsum("ocq,dq->ocd", du8, parent_grid, preferred_element_type=jnp.float32)
    delta_parent = jnp.einsum(
        "ocd,ocq->dq", up_weight, du8, preferred_element_type=jnp.float32
    ).astype(jnp.bfloat16)
    slot_grad = lax.dot_general(
        delta_parent, onehot, (((1,), (1,)), ((), ())), preferred_element_type=jnp.float32
    ).astype(jnp.bfloat16)
    returned = lax.all_to_all(slot_grad, ("gz", "xy"), split_axis=1, concat_axis=1, tiled=True)
    grad_parent = jnp.where(live[None, :], returned, jnp.zeros_like(returned))[None]
    sum_one, sum_two, sum_up = lax.psum((term_one, term_two, term_up), ("gz", "xy"))
    scale = 1.0 / math.sqrt(size_x * count_xy * size_y * size_z * count_gz)
    return (decoded, grad_parent, sum_one * scale, sum_two * scale, sum_up * scale)


def solution(mesh):
    placed = (
        P(("gz", "xy"), None, None),
        P(("gz", "xy"), None),
        P(("gz", "xy"), None),
        P(),
        P(),
        P(),
        P("xy", None, "gz"),
        P(None, "xy", None, "gz"),
    )
    return jax.shard_map(
        local,
        mesh=mesh,
        in_specs=placed,
        out_specs=(P(None, "xy", None, "gz"), P(("gz", "xy"), None, None), P(), P(), P()),
        check_vma=False,
    )
```

profile of v0, /device:TPU:1, one launch (start us, length us, event | category | flops | bytes accessed | tf_op | source)
XLA Modules:
  0.0 432.3 jit_solution(10108309760339999828)
XLA Ops:
  7.7 1.4 reduce.6
  9.8 11.5 %all-to-all-start.1 = ((s32[1,128,16]{2,0,1:T(1,128)}), s32[1,128,16]{2,0,1:T(1,128)S(1)}, u32[]{:S(2)}, u32[]{:S(2)}) async-start(s32[1,128,16]{2,0,1:T(1,128)} %bitcast.3), calls=%async_computation.1 | async-start | bytes 131072 | tf_op jit(solution)/shard_map/all_to_all | solution.py:86
  22.0 1.2 copy.273
  24.6 6.2 %all-to-all-done.1 = s32[1,128,16]{2,0,1:T(1,128)S(1)} async-done(((s32[1,128,16]{2,0,1:T(1,128)}), s32[1,128,16]{2,0,1:T(1,128)S(1)}, u32[]{:S(2)}, u32[]{:S(2)}) %all-to-all-start.1) | async-done | bytes 8224 | tf_op jit(solution)/shard_map/all_to_all | solution.py:86
  30.8 4.5 %all-to-all-start = ((bf16[128,2,512]{2,1,0:T(2,128)(2,1)}), bf16[128,2,512]{2,1,0:T(2,128)(2,1)S(1)}, u32[]{:S(2)}, u32[]{:S(2)}) async-start(bf16[128,2,512]{2,1,0:T(2,128)(2,1)} %reshape.685), calls=%async_computation | async-start | bytes 524288 | tf_op jit(solution)/shard_map/all_to_all | solution.py:85
  36.8 9.8 %all-to-all-done = bf16[128,2,512]{2,1,0:T(2,128)(2,1)S(1)} async-done(((bf16[128,2,512]{2,1,0:T(2,128)(2,1)}), bf16[128,2,512]{2,1,0:T(2,128)(2,1)S(1)}, u32[]{:S(2)}, u32[]{:S(2)}) %all-to-all-start) | async-done | bytes 262176 | tf_op jit(solution)/shard_map/all_to_all | solution.py:85
  49.3 2.5 collective-permute-start
  51.8 1.3 collective-permute-start.1
  53.9 3.6 collective-permute-done.1
  57.8 4.3 collective-permute-start.2
  62.1 1.9 collective-permute-start.3
  64.0 1.7 fusion.118
  65.7 2.5 collective-permute-done.2
  68.2 4.4 %collective-permute-done.3 = bf16[64,4,8,1]{3,0,2,1:T(8,128)(2,1)S(1)} collective-permute-done((bf16[64,4,8,1]{3,0,2,1:T(8,128)(2,1)S(1)}, bf16[64,4,8,1]{3,0,2,1:T(8,128)(2,1)S(1)}, u32[]{:S(2)}, u32[]{:S(2)}) %collective-permute-start.3) | collective-permute-done | bytes 4128 | tf_op jit(solution)/shard_map/ppermute | solution.py:18
  73.2 1.2 fusion.605
  92.9 2.0 collective-permute-start.4
  94.9 1.3 collective-permute-start.5
  96.8 3.8 collective-permute-done.5
  101.4 1.2 fusion.608
  102.5 4.1 collective-permute-start.6
  106.7 2.5 collective-permute-start.7
  110.8 2.3 collective-permute-done.6
  113.1 4.4 %collective-permute-done.7 = bf16[64,4,8,1]{3,0,2,1:T(8,128)(2,1)} collective-permute-done((bf16[64,4,8,1]{3,0,2,1:T(8,128)(2,1)}, bf16[64,4,8,1]{3,0,2,1:T(8,128)(2,1)}, u32[]{:S(2)}, u32[]{:S(2)}) %collective-permute-start.7) | collective-permute-done | bytes 4128 | tf_op jit(solution)/shard_map/ppermute | solution.py:18
  117.5 1.9 select_maximum_fusion.8
  119.4 1.2 fusion.604
  121.6 1.5 pad_maximum_fusion.36
  123.3 1.7 pad_maximum_fusion.35
  141.8 1.2 multiply_convert_fusion.2
  149.3 5.2 %collective-permute-start.8 = (bf16[64,1,8,128]{3,0,2,1:T(8,128)(2,1)S(1)}, bf16[64,1,8,128]{3,0,2,1:T(8,128)(2,1)S(1)}, u32[]{:S(2)}, u32[]{:S(2)}) collective-permute-start(bf16[64,1,8,128]{3,0,2,1:T(8,128)(2,1)S(1)} %get-tuple-element.144), channel_id=1, source_target_pairs={{0,1},{1,2},{2,3},{3,4},{4,5},{5,6},{6,7},{7,8},{8,9},{9,10},{10,1... | collective-permute-start | bytes 393224 | tf_op jit(solution)/shard_map/ppermute | solution.py:17
  154.5 1.3 collective-permute-start.9
  156.4 3.8 collective-permute-done.9
  160.6 3.8 collective-permute-start.10
  164.4 1.9 collective-permute-start.11
  166.8 3.7 collective-permute-done.10
  170.5 4.4 %collective-permute-done.11 = bf16[64,4,8,1]{3,0,2,1:T(8,128)(2,1)S(1)} collective-permute-done((bf16[64,4,8,1]{3,0,2,1:T(8,128)(2,1)S(1)}, bf16[64,4,8,1]{3,0,2,1:T(8,128)(2,1)S(1)}, u32[]{:S(2)}, u32[]{:S(2)}) %collective-permute-start.11) | collective-permute-done | bytes 4128 | tf_op jit(solution)/shard_map/ppermute | solution.py:18
  175.5 1.3 fusion.603
  184.1 1.0 convolution_bitcast_fusion.31
  185.3 1.0 convolution_bitcast_fusion.32
  186.5 1.0 convolution_bitcast_fusion.36
  188.8 1.0 convolution_bitcast_fusion.38
  190.0 1.0 convolution_bitcast_fusion.39
  195.3 1.0 multiply_convert_fusion.1
  203.5 3.5 collective-permute-start.12
  207.0 1.3 collective-permute-start.13
  208.9 3.8 collective-permute-done.13
  213.0 4.1 collective-permute-start.14
  217.2 1.9 collective-permute-start.15
  219.4 3.9 collective-permute-done.14
  223.3 4.4 %collective-permute-done.15 = bf16[64,4,8,1]{3,0,2,1:T(8,128)(2,1)S(1)} collective-permute-done((bf16[64,4,8,1]{3,0,2,1:T(8,128)(2,1)S(1)}, bf16[64,4,8,1]{3,0,2,1:T(8,128)(2,1)S(1)}, u32[]{:S(2)}, u32[]{:S(2)}) %collective-permute-start.15) | collective-permute-done | bytes 4128 | tf_op jit(solution)/shard_map/ppermute | solution.py:18
  228.4 1.1 fusion.602
  238.1 1.0 convolution_bitcast_fusion.24
  239.2 1.0 convolution_bitcast_fusion.20
  240.4 1.0 convolution_bitcast_fusion.21
  241.6 1.0 convolution_bitcast_fusion.22
  242.8 1.0 convolution_bitcast_fusion.26
  243.9 1.0 convolution_bitcast_fusion.27
  246.3 1.0 convolution_bitcast_fusion.29
  249.6 1.4 fusion.121
  252.7 1.0 reshape.687
  253.7 7.1 %all-to-all-start.2 = ((bf16[128,2,512]{2,1,0:T(2,128)(2,1)}), bf16[128,2,512]{2,1,0:T(2,128)(2,1)S(1)}, u32[]{:S(2)}, u32[]{:S(2)}) async-start(bf16[128,2,512]{2,1,0:T(2,128)(2,1)} %reshape.687), calls=%async_computation.2 | async-start | bytes 524288 | tf_op jit(solution)/shard_map/all_to_all | solution.py:127
  262.7 9.3 %all-to-all-done.2 = bf16[128,2,512]{2,1,0:T(2,128)(2,1)S(1)} async-done(((bf16[128,2,512]{2,1,0:T(2,128)(2,1)}), bf16[128,2,512]{2,1,0:T(2,128)(2,1)S(1)}, u32[]{:S(2)}, u32[]{:S(2)}) %all-to-all-start.2) | async-done | bytes 262176 | tf_op jit(solution)/shard_map/all_to_all | solution.py:127
  273.6 147.1 %all-reduce.7.cloned.1.call-done = (f32[27,64,64]{2,1,0:T(8,128)}, f32[27,64,64]{2,1,0:T(8,128)}, f32[8,64,64]{2,1,0:T(8,128)}) async-done(((f32[27,64,64]{2,1,0:T(8,128)}, f32[27,64,64]{2,1,0:T(8,128)}, f32[8,64,64]{2,1,0:T(8,128)}), (f32[27,64,64]{2,1,0:T(8,128)}, f32[27,64,64]{2,1,0:T(8,128)}, f32[8,64,64]{2,1,0:T(8,128)})) %all-reduce.7.cloned.1.call-update) | async-done | bytes 1015824 | tf_op jit(solution)/shard_map/psum | solution.py:129
  420.7 1.7 broadcast_multiply_fusion.2
  422.4 2.9 broadcast_multiply_fusion
  (389 shorter events, 96.2 us)
Async XLA Ops:
  7.2 40.4 %copy-start = (bf16[8,64,64]{2,1,0:T(8,128)(2,1)S(1)}, bf16[8,64,64]{2,1,0:T(8,128)(2,1)}, u32[]{:S(2)}) copy-start(bf16[8,64,64]{2,1,0:T(8,128)(2,1)} %param.11) | copy-start | bytes 196612
  9.8 21.0 %all-to-all-start.1 = ((s32[1,128,16]{2,0,1:T(1,128)}), s32[1,128,16]{2,0,1:T(1,128)S(1)}, u32[]{:S(2)}, u32[]{:S(2)}) async-start(s32[1,128,16]{2,0,1:T(1,128)} %bitcast.3), calls=%async_computation.1 | async-start | bytes 131072 | tf_op jit(solution)/shard_map/all_to_all | solution.py:86
  23.2 12.0 %copy-start.33 = (s32[2,8,128]{2,1,0:T(8,128)S(1)}, s32[2,8,128]{2,1,0:T(8,128)}, u32[]{:S(2)}) copy-start(s32[2,8,128]{2,1,0:T(8,128)} %param.14) | copy-start | bytes 24580
  30.8 15.7 %all-to-all-start = ((bf16[128,2,512]{2,1,0:T(2,128)(2,1)}), bf16[128,2,512]{2,1,0:T(2,128)(2,1)S(1)}, u32[]{:S(2)}, u32[]{:S(2)}) async-start(bf16[128,2,512]{2,1,0:T(2,128)(2,1)} %reshape.685), calls=%async_computation | async-start | bytes 524288 | tf_op jit(solution)/shard_map/all_to_all | solution.py:85
  36.8 10.1 %copy-start.34 = (s32[2048]{0:T(1024)}, s32[2048]{0:T(1024)S(1)}, u32[]{:S(2)}) copy-start(s32[2048]{0:T(1024)S(1)} %eq.17) | copy-start | bytes 24580
  47.6 1.3 copy-start.30
  49.3 4.6 %collective-permute-start = (bf16[64,1,8,128]{3,0,2,1:T(8,128)(2,1)S(1)}, bf16[64,1,8,128]{3,0,2,1:T(8,128)(2,1)S(1)}, u32[]{:S(2)}, u32[]{:S(2)}) collective-permute-start(bf16[64,1,8,128]{3,0,2,1:T(8,128)(2,1)S(1)} %get-tuple-element.148), channel_id=1, source_target_pairs={{0,1},{1,2},{2,3},{3,4},{4,5},{5,6},{6,7},{7,8},{8,9},{9,10},{10,1... | collective-permute-start | bytes 393224 | tf_op jit(solution)/shard_map/ppermute | solution.py:17
  51.8 5.7 %collective-permute-start.1 = (bf16[64,1,8,128]{3,0,2,1:T(8,128)(2,1)S(1)}, bf16[64,1,8,128]{3,0,2,1:T(8,128)(2,1)S(1)}, u32[]{:S(2)}, u32[]{:S(2)}) collective-permute-start(bf16[64,1,8,128]{3,0,2,1:T(8,128)(2,1)S(1)} %get-tuple-element.149), channel_id=1, source_target_pairs={{1,0},{2,1},{3,2},{4,3},{5,4},{6,5},{7,6},{8,7},{9,8},{10,9},{11,1... | collective-permute-start | bytes 393224 | tf_op jit(solution)/shard_map/ppermute | solution.py:18
  53.6 10.4 %copy-start.1 = (f32[2,4,2,64,2]{4,3,2,1,0:T(8,128)}, f32[2,4,2,64,2]{4,3,2,1,0:T(8,128)S(1)}, u32[]{:S(2)}) copy-start(f32[2,4,2,64,2]{4,3,2,1,0:T(8,128)S(1)} %mul.119) | copy-start | bytes 24580
  53.9 18.7 %copy-start.17 = (bf16[64,1,8,128]{3,0,2,1:T(8,128)(2,1)}, bf16[64,1,8,128]{3,0,2,1:T(8,128)(2,1)S(1)}, u32[]{:S(2)}) copy-start(bf16[64,1,8,128]{3,0,2,1:T(8,128)(2,1)S(1)} %collective-permute-done) | copy-start | bytes 393220
  57.8 10.4 %collective-permute-start.2 = (bf16[64,4,8,1]{3,0,2,1:T(8,128)(2,1)S(1)}, bf16[64,4,8,1]{3,0,2,1:T(8,128)(2,1)S(1)}, u32[]{:S(2)}, u32[]{:S(2)}) collective-permute-start(bf16[64,4,8,1]{3,0,2,1:T(8,128)(2,1)S(1)} %get-tuple-element.132), channel_id=1, source_target_pairs={{0,16},{16,32},{32,48},{48,64},{64,80},{80,96},{96,112},{1,17},{17... | collective-permute-start | bytes 12296 | tf_op jit(solution)/shard_map/ppermute | solution.py:17
  62.1 10.5 %collective-permute-start.3 = (bf16[64,4,8,1]{3,0,2,1:T(8,128)(2,1)S(1)}, bf16[64,4,8,1]{3,0,2,1:T(8,128)(2,1)S(1)}, u32[]{:S(2)}, u32[]{:S(2)}) collective-permute-start(bf16[64,4,8,1]{3,0,2,1:T(8,128)(2,1)S(1)} %get-tuple-element.133), channel_id=1, source_target_pairs={{16,0},{32,16},{48,32},{64,48},{80,64},{96,80},{112,96},{17,1},{33... | collective-permute-start | bytes 12296 | tf_op jit(solution)/shard_map/ppermute | solution.py:18
  74.5 0.9 copy-start.18
  75.7 0.7 copy-start.11
  75.7 2.9 copy-start.9
  77.1 1.0 copy-start.13
  77.2 1.0 copy-start.15
  77.2 1.7 copy-start.7
  77.2 10.4 %copy-start.3 = (bf16[64,2,8,128]{3,0,2,1:T(8,128)(2,1)}, bf16[64,2,8,128]{3,0,2,1:T(8,128)(2,1)S(1)}, u32[]{:S(2)}) copy-start(bf16[64,2,8,128]{3,0,2,1:T(8,128)(2,1)S(1)} %get-tuple-element.120) | copy-start | bytes 786436
  77.2 10.8 %copy-start.5 = (bf16[64,2,8,128]{3,0,2,1:T(8,128)(2,1)}, bf16[64,2,8,128]{3,0,2,1:T(8,128)(2,1)S(1)}, u32[]{:S(2)}) copy-start(bf16[64,2,8,128]{3,0,2,1:T(8,128)(2,1)S(1)} %get-tuple-element.141) | copy-start | bytes 786436
  78.5 1.0 copy-start.23
  92.9 3.9 collective-permute-start.4
  94.9 5.7 %collective-permute-start.5 = (bf16[64,1,8,128]{3,0,2,1:T(8,128)(2,1)S(1)}, bf16[64,1,8,128]{3,0,2,1:T(8,128)(2,1)S(1)}, u32[]{:S(2)}, u32[]{:S(2)}) collective-permute-start(bf16[64,1,8,128]{3,0,2,1:T(8,128)(2,1)S(1)} %get-tuple-element.147), channel_id=1, source_target_pairs={{1,0},{2,1},{3,2},{4,3},{5,4},{6,5},{7,6},{8,7},{9,8},{10,9},{11,1... | collective-permute-start | bytes 393224 | tf_op jit(solution)/shard_map/ppermute | solution.py:18
  96.8 3.8 copy-start.19
  100.6 0.7 copy-start.21
  101.4 7.8 %copy-start.36 = (s32[1,128]{1,0:T(1,128)S(1)}, s32[1,128]{1,0:T(1,128)}, u32[]{:S(2)}) copy-start(s32[1,128]{1,0:T(1,128)} %param.10) | copy-start | bytes 1540
  102.5 10.6 %collective-permute-start.6 = (bf16[64,4,8,1]{3,0,2,1:T(8,128)(2,1)}, bf16[64,4,8,1]{3,0,2,1:T(8,128)(2,1)}, u32[]{:S(2)}, u32[]{:S(2)}) collective-permute-start(bf16[64,4,8,1]{3,0,2,1:T(8,128)(2,1)} %get-tuple-element.130), channel_id=1, source_target_pairs={{0,16},{16,32},{32,48},{48,64},{64,80},{80,96},{96,112},{1,17},{17... | collective-permute-start | bytes 12296 | tf_op jit(solution)/shard_map/ppermute | solution.py:17
  106.7 10.8 %collective-permute-start.7 = (bf16[64,4,8,1]{3,0,2,1:T(8,128)(2,1)}, bf16[64,4,8,1]{3,0,2,1:T(8,128)(2,1)}, u32[]{:S(2)}, u32[]{:S(2)}) collective-permute-start(bf16[64,4,8,1]{3,0,2,1:T(8,128)(2,1)} %get-tuple-element.131), channel_id=1, source_target_pairs={{16,0},{32,16},{48,32},{64,48},{80,64},{96,80},{112,96},{17,1},{33... | collective-permute-start | bytes 12296 | tf_op jit(solution)/shard_map/ppermute | solution.py:18
  120.6 0.9 copy-start.20
  120.6 1.0 copy-start.22
  126.2 1.0 copy-start.25
  139.4 0.7 copy-start.32
  140.9 1.0 copy-start.29
  149.3 7.2 %collective-permute-start.8 = (bf16[64,1,8,128]{3,0,2,1:T(8,128)(2,1)S(1)}, bf16[64,1,8,128]{3,0,2,1:T(8,128)(2,1)S(1)}, u32[]{:S(2)}, u32[]{:S(2)}) collective-permute-start(bf16[64,1,8,128]{3,0,2,1:T(8,128)(2,1)S(1)} %get-tuple-element.144), channel_id=1, source_target_pairs={{0,1},{1,2},{2,3},{3,4},{4,5},{5,6},{6,7},{7,8},{8,9},{9,10},{10,1... | collective-permute-start | bytes 393224 | tf_op jit(solution)/shard_map/ppermute | solution.py:17
  154.5 5.7 %collective-permute-start.9 = (bf16[64,1,8,128]{3,0,2,1:T(8,128)(2,1)S(1)}, bf16[64,1,8,128]{3,0,2,1:T(8,128)(2,1)S(1)}, u32[]{:S(2)}, u32[]{:S(2)}) collective-permute-start(bf16[64,1,8,128]{3,0,2,1:T(8,128)(2,1)S(1)} %get-tuple-element.145), channel_id=1, source_target_pairs={{1,0},{2,1},{3,2},{4,3},{5,4},{6,5},{7,6},{8,7},{9,8},{10,9},{11,1... | collective-permute-start | bytes 393224 | tf_op jit(solution)/shard_map/ppermute | solution.py:18
  160.6 9.9 %collective-permute-start.10 = (bf16[64,4,8,1]{3,0,2,1:T(8,128)(2,1)S(1)}, bf16[64,4,8,1]{3,0,2,1:T(8,128)(2,1)S(1)}, u32[]{:S(2)}, u32[]{:S(2)}) collective-permute-start(bf16[64,4,8,1]{3,0,2,1:T(8,128)(2,1)S(1)} %get-tuple-element.128), channel_id=1, source_target_pairs={{0,16},{16,32},{32,48},{48,64},{64,80},{80,96},{96,112},{1,17},{17... | collective-permute-start | bytes 12296 | tf_op jit(solution)/shard_map/ppermute | solution.py:17
  164.4 10.5 %collective-permute-start.11 = (bf16[64,4,8,1]{3,0,2,1:T(8,128)(2,1)S(1)}, bf16[64,4,8,1]{3,0,2,1:T(8,128)(2,1)S(1)}, u32[]{:S(2)}, u32[]{:S(2)}) collective-permute-start(bf16[64,4,8,1]{3,0,2,1:T(8,128)(2,1)S(1)} %get-tuple-element.129), channel_id=1, source_target_pairs={{16,0},{32,16},{48,32},{64,48},{80,64},{96,80},{112,96},{17,1},{33... | collective-permute-start | bytes 12296 | tf_op jit(solution)/shard_map/ppermute | solution.py:18
  166.6 3.9 copy-start.27
  196.8 1.0 copy-start.12
  196.9 1.2 copy-start.16
  197.1 1.1 copy-start.14
  198.7 1.4 copy-start.10
  199.8 1.0 copy-start.8
  201.5 1.4 copy-start.6
  201.8 1.3 copy-start.4
  203.5 5.4 %collective-permute-start.12 = (bf16[64,1,8,128]{3,0,2,1:T(8,128)(2,1)S(1)}, bf16[64,1,8,128]{3,0,2,1:T(8,128)(2,1)S(1)}, u32[]{:S(2)}, u32[]{:S(2)}) collective-permute-start(bf16[64,1,8,128]{3,0,2,1:T(8,128)(2,1)S(1)} %get-tuple-element.142), channel_id=1, source_target_pairs={{0,1},{1,2},{2,3},{3,4},{4,5},{5,6},{6,7},{7,8},{8,9},{9,10},{10,1... | collective-permute-start | bytes 393224 | tf_op jit(solution)/shard_map/ppermute | solution.py:17
  207.0 5.7 %collective-permute-start.13 = (bf16[64,1,8,128]{3,0,2,1:T(8,128)(2,1)S(1)}, bf16[64,1,8,128]{3,0,2,1:T(8,128)(2,1)S(1)}, u32[]{:S(2)}, u32[]{:S(2)}) collective-permute-start(bf16[64,1,8,128]{3,0,2,1:T(8,128)(2,1)S(1)} %get-tuple-element.143), channel_id=1, source_target_pairs={{1,0},{2,1},{3,2},{4,3},{5,4},{6,5},{7,6},{8,7},{9,8},{10,9},{11,1... | collective-permute-start | bytes 393224 | tf_op jit(solution)/shard_map/ppermute | solution.py:18
  213.0 10.2 %collective-permute-start.14 = (bf16[64,4,8,1]{3,0,2,1:T(8,128)(2,1)S(1)}, bf16[64,4,8,1]{3,0,2,1:T(8,128)(2,1)S(1)}, u32[]{:S(2)}, u32[]{:S(2)}) collective-permute-start(bf16[64,4,8,1]{3,0,2,1:T(8,128)(2,1)S(1)} %get-tuple-element.126), channel_id=1, source_target_pairs={{0,16},{16,32},{32,48},{48,64},{64,80},{80,96},{96,112},{1,17},{17... | collective-permute-start | bytes 12296 | tf_op jit(solution)/shard_map/ppermute | solution.py:17
  217.2 10.5 %collective-permute-start.15 = (bf16[64,4,8,1]{3,0,2,1:T(8,128)(2,1)S(1)}, bf16[64,4,8,1]{3,0,2,1:T(8,128)(2,1)S(1)}, u32[]{:S(2)}, u32[]{:S(2)}) collective-permute-start(bf16[64,4,8,1]{3,0,2,1:T(8,128)(2,1)S(1)} %get-tuple-element.127), channel_id=1, source_target_pairs={{16,0},{32,16},{48,32},{64,48},{80,64},{96,80},{112,96},{17,1},{33... | collective-permute-start | bytes 12296 | tf_op jit(solution)/shard_map/ppermute | solution.py:18
  219.4 8.9 %copy-start.28 = (f32[27,64,64]{2,1,0:T(8,128)}, f32[27,64,64]{2,1,0:T(8,128)S(1)}, u32[]{:S(2)}) copy-start(f32[27,64,64]{2,1,0:T(8,128)S(1)} %fusion.92) | copy-start | bytes 1327108
  228.3 1.3 copy-start.24
  248.6 1.0 copy-start.2
  251.0 0.9 copy-start.35
  252.5 8.4 %copy-start.31 = (bf16[64,256,1]{1,0,2:T(8,128)(2,1)S(1)}, bf16[64,256,1]{1,0,2:T(8,128)(2,1)}, u32[]{:S(2)}) copy-start(bf16[64,256,1]{1,0,2:T(8,128)(2,1)} %copy-done.30) | copy-start | bytes 98308
  253.7 18.3 %all-to-all-start.2 = ((bf16[128,2,512]{2,1,0:T(2,128)(2,1)}), bf16[128,2,512]{2,1,0:T(2,128)(2,1)S(1)}, u32[]{:S(2)}, u32[]{:S(2)}) async-start(bf16[128,2,512]{2,1,0:T(2,128)(2,1)} %reshape.687), calls=%async_computation.2 | async-start | bytes 524288 | tf_op jit(solution)/shard_map/all_to_all | solution.py:127
  260.8 1.0 copy-start.26
  260.8 159.9 %all-reduce.7.cloned.1.call-start = ((), (), s32[]{:S(2)}) async-start(), calls=%async_computation.3 | async-start | bytes 4063232 | tf_op jit(solution)/shard_map/psum | solution.py:129
Sparse Core Ops, SparseCore 0:
  267.6 153.0 all-reduce.6
where the time goes:
time: 441 us; the launch traced here: 432 us
  waiting for transfers between devices  219 us (50%)
  starting transfers between devices  66 us (15%)
  matrix products  65.7 us (15%)
  local copies, waits for them, and re-layouts  41.5 us (9%)
  other arithmetic  23.5 us (5%)
  between operations  16.7 us (4%)
    psum x1, waiting for transfers between devices, local(): lax.psum((term_one, term_two, term_up), ('gz', 'xy'))  147 us
    dot_general x108, matrix products, convolve(): jnp.dot(orient(weights[index], direction), window(padded, offset, directi...  50.1 us
    ppermute x8, waiting for transfers between devices, with_halo(): after = lax.ppermute(first, axis, down)  32.5 us
    ppermute x8, starting transfers between devices, with_halo(): before = lax.ppermute(last, axis, up)  29.5 us
    slice x108, local copies, waits for them, and re-layouts, window(): part = padded[:, 1 + ox:1 + ox + nx, 1 + oy:1 + oy + ny, 1 + oz:1 + oz + nz]  23.1 us
    ppermute x8, waiting for transfers between devices, with_halo(): before = lax.ppermute(last, axis, up)  13.9 us
    ppermute x8, starting transfers between devices, with_halo(): after = lax.ppermute(first, axis, down)  13.4 us
    dot_general x54, matrix products, weight_terms(): lax.dot_general(flat, window(padded, offset, 1, shape), (((1,), (1,)), ((...  13.2 us
  transfers between devices with their start and end apart: 20, of which 20 were waited for; matrix products, arithmetic and copies ran while one was open for 3% of the time, Pallas kernels for 0%

commit v1 on v0

--- a/solution.py
+++ b/solution.py
@@ -126,7 +126,7 @@
     ).astype(jnp.bfloat16)
     returned = lax.all_to_all(slot_grad, ("gz", "xy"), split_axis=1, concat_axis=1, tiled=True)
     grad_parent = jnp.where(live[None, :], returned, jnp.zeros_like(returned))[None]
-    sum_one, sum_two, sum_up = lax.psum((term_one, term_two, term_up), ("gz", "xy"))
+    sum_one, sum_two, sum_up = lax.psum(lax.psum((term_one, term_two, term_up), "gz"), "xy")
     scale = 1.0 / math.sqrt(size_x * count_xy * size_y * size_z * count_gz)
     return (decoded, grad_parent, sum_one * scale, sum_two * scale, sum_up * scale)
 

time: 441 us -> 424 us (0.961)
  the two profiles are of different devices: /device:TPU:1 before, /device:TPU:0 now
where the time goes in v1:
time: 424 us; the launch traced here: 415 us
  waiting for transfers between devices  204 us (48%)
  starting transfers between devices  73.9 us (17%)
  matrix products  65.8 us (16%)
  local copies, waits for them, and re-layouts  36.6 us (9%)
  other arithmetic  18.7 us (4%)
  between operations  16.4 us (4%)
    psum x1, waiting for transfers between devices, local(): lax.psum(lax.psum((term_one, term_two, term_up), 'gz'), 'xy')  73.5 us
    psum x1, waiting for transfers between devices, local(): lax.psum((term_one, term_two, term_up), 'gz')  71.8 us
    dot_general x108, matrix products, convolve(): jnp.dot(orient(weights[index], direction), window(padded, offset, directi...  50.2 us
    ppermute x8, starting transfers between devices, with_halo(): before = lax.ppermute(last, axis, up)  38.7 us
    ppermute x8, waiting for transfers between devices, with_halo(): after = lax.ppermute(first, axis, down)  29 us
    slice x108, local copies, waits for them, and re-layouts, window(): part = padded[:, 1 + ox:1 + ox + nx, 1 + oy:1 + oy + ny, 1 + oz:1 + oz + nz]  23.1 us
    dot_general x54, matrix products, weight_terms(): lax.dot_general(flat, window(padded, offset, 1, shape), (((1,), (1,)), ((...  13.2 us
    all_to_all x1, starting transfers between devices, local(): lax.all_to_all(parent_cell, ('gz', 'xy'), split_axis=1, concat_axis=1, ti...  11.2 us
  transfers between devices with their start and end apart: 21, of which 17 were waited for; matrix products, arithmetic and copies ran while one was open for 3% of the time, Pallas kernels for 0%

profile of v1, /device:TPU:0, one launch (start us, length us, event | category | flops | bytes accessed | tf_op | source)
XLA Modules:
  0.0 415.4 jit_solution(8600361435045094774)
XLA Ops:
  7.7 1.4 reduce.6
  9.8 11.2 %all-to-all-start.1 = ((s32[1,128,16]{2,0,1:T(1,128)}), s32[1,128,16]{2,0,1:T(1,128)S(1)}, u32[]{:S(2)}, u32[]{:S(2)}) async-start(s32[1,128,16]{2,0,1:T(1,128)} %bitcast.3), calls=%async_computation.1 | async-start | bytes 131072 | tf_op jit(solution)/shard_map/all_to_all | solution.py:86
  21.7 1.2 copy.273
  23.3 1.0 reshape.685
  24.3 6.1 %all-to-all-done.1 = s32[1,128,16]{2,0,1:T(1,128)S(1)} async-done(((s32[1,128,16]{2,0,1:T(1,128)}), s32[1,128,16]{2,0,1:T(1,128)S(1)}, u32[]{:S(2)}, u32[]{:S(2)}) %all-to-all-start.1) | async-done | bytes 8224 | tf_op jit(solution)/shard_map/all_to_all | solution.py:86
  30.4 4.6 %all-to-all-start = ((bf16[128,2,512]{2,1,0:T(2,128)(2,1)}), bf16[128,2,512]{2,1,0:T(2,128)(2,1)S(1)}, u32[]{:S(2)}, u32[]{:S(2)}) async-start(bf16[128,2,512]{2,1,0:T(2,128)(2,1)} %reshape.685), calls=%async_computation | async-start | bytes 524288 | tf_op jit(solution)/shard_map/all_to_all | solution.py:85
  36.0 9.9 %all-to-all-done = bf16[128,2,512]{2,1,0:T(2,128)(2,1)S(1)} async-done(((bf16[128,2,512]{2,1,0:T(2,128)(2,1)}), bf16[128,2,512]{2,1,0:T(2,128)(2,1)S(1)}, u32[]{:S(2)}, u32[]{:S(2)}) %all-to-all-start) | async-done | bytes 262176 | tf_op jit(solution)/shard_map/all_to_all | solution.py:85
  48.6 2.7 collective-permute-start
  51.4 1.3 collective-permute-start.1
  54.1 4.2 %collective-permute-done.1 = bf16[64,1,8,128]{3,0,2,1:T(8,128)(2,1)S(1)} collective-permute-done((bf16[64,1,8,128]{3,0,2,1:T(8,128)(2,1)S(1)}, bf16[64,1,8,128]{3,0,2,1:T(8,128)(2,1)S(1)}, u32[]{:S(2)}, u32[]{:S(2)}) %collective-permute-start.1) | collective-permute-done | bytes 131104 | tf_op jit(solution)/shard_map/ppermute | solution.py:18
  58.6 1.3 collective-permute-start.2
  59.9 1.3 collective-permute-start.3
  61.2 1.7 fusion.118
  62.9 1.6 collective-permute-done.3
  65.2 1.3 fusion.605
  71.6 0.9 convolution_bitcast_fusion.11
  72.7 0.9 convolution_bitcast_fusion.12
  83.8 2.3 collective-permute-start.4
  86.0 1.3 collective-permute-start.5
  87.3 1.2 collective-permute-done.4
  88.5 4.4 %collective-permute-done.5 = bf16[64,1,8,128]{3,0,2,1:T(8,128)(2,1)S(1)} collective-permute-done((bf16[64,1,8,128]{3,0,2,1:T(8,128)(2,1)S(1)}, bf16[64,1,8,128]{3,0,2,1:T(8,128)(2,1)S(1)}, u32[]{:S(2)}, u32[]{:S(2)}) %collective-permute-start.5) | collective-permute-done | bytes 131104 | tf_op jit(solution)/shard_map/ppermute | solution.py:18
  93.2 7.7 %collective-permute-start.6 = (bf16[64,4,8,1]{3,0,2,1:T(8,128)(2,1)S(1)}, bf16[64,4,8,1]{3,0,2,1:T(8,128)(2,1)S(1)}, u32[]{:S(2)}, u32[]{:S(2)}) collective-permute-start(bf16[64,4,8,1]{3,0,2,1:T(8,128)(2,1)S(1)} %get-tuple-element.133), channel_id=1, source_target_pairs={{0,16},{16,32},{32,48},{48,64},{64,80},{80,96},{96,112},{1,17},{17... | collective-permute-start | bytes 12296 | tf_op jit(solution)/shard_map/ppermute | solution.py:17
  100.9 1.9 collective-permute-start.7
  102.8 3.6 collective-permute-done.7
  107.1 1.2 fusion.604
  133.3 5.5 %collective-permute-start.8 = (bf16[64,1,8,128]{3,0,2,1:T(8,128)(2,1)S(1)}, bf16[64,1,8,128]{3,0,2,1:T(8,128)(2,1)S(1)}, u32[]{:S(2)}, u32[]{:S(2)}) collective-permute-start(bf16[64,1,8,128]{3,0,2,1:T(8,128)(2,1)S(1)} %get-tuple-element.147), channel_id=1, source_target_pairs={{0,1},{1,2},{2,3},{3,4},{4,5},{5,6},{6,7},{7,8},{8,9},{9,10},{10,1... | collective-permute-start | bytes 393224 | tf_op jit(solution)/shard_map/ppermute | solution.py:17
  138.8 1.3 collective-permute-start.9
  141.3 4.4 %collective-permute-done.9 = bf16[64,1,8,128]{3,0,2,1:T(8,128)(2,1)S(1)} collective-permute-done((bf16[64,1,8,128]{3,0,2,1:T(8,128)(2,1)S(1)}, bf16[64,1,8,128]{3,0,2,1:T(8,128)(2,1)S(1)}, u32[]{:S(2)}, u32[]{:S(2)}) %collective-permute-start.9) | collective-permute-done | bytes 131104 | tf_op jit(solution)/shard_map/ppermute | solution.py:18
  146.0 7.7 %collective-permute-start.10 = (bf16[64,4,8,1]{3,0,2,1:T(8,128)(2,1)S(1)}, bf16[64,4,8,1]{3,0,2,1:T(8,128)(2,1)S(1)}, u32[]{:S(2)}, u32[]{:S(2)}) collective-permute-start(bf16[64,4,8,1]{3,0,2,1:T(8,128)(2,1)S(1)} %get-tuple-element.131), channel_id=1, source_target_pairs={{0,16},{16,32},{32,48},{48,64},{64,80},{80,96},{96,112},{1,17},{17... | collective-permute-start | bytes 12296 | tf_op jit(solution)/shard_map/ppermute | solution.py:17
  153.7 1.3 collective-permute-start.11
  156.2 2.6 collective-permute-done.11
  159.5 1.2 fusion.603
  165.7 1.0 convolution_bitcast_fusion.34
  166.9 1.0 convolution_bitcast_fusion.30
  168.0 1.0 convolution_bitcast_fusion.31
  169.2 1.0 convolution_bitcast_fusion.32
  170.4 1.0 convolution_bitcast_fusion.36
  171.6 1.0 convolution_bitcast_fusion.37
  172.7 1.0 convolution_bitcast_fusion.38
  173.9 1.0 convolution_bitcast_fusion.39
  179.2 1.1 multiply_convert_fusion.1
  187.1 3.8 collective-permute-start.12
  190.9 1.3 collective-permute-start.13
  193.4 4.4 %collective-permute-done.13 = bf16[64,1,8,128]{3,0,2,1:T(8,128)(2,1)S(1)} collective-permute-done((bf16[64,1,8,128]{3,0,2,1:T(8,128)(2,1)S(1)}, bf16[64,1,8,128]{3,0,2,1:T(8,128)(2,1)S(1)}, u32[]{:S(2)}, u32[]{:S(2)}) %collective-permute-start.13) | collective-permute-done | bytes 131104 | tf_op jit(solution)/shard_map/ppermute | solution.py:18
  198.0 7.7 %collective-permute-start.14 = (bf16[64,4,8,1]{3,0,2,1:T(8,128)(2,1)S(1)}, bf16[64,4,8,1]{3,0,2,1:T(8,128)(2,1)S(1)}, u32[]{:S(2)}, u32[]{:S(2)}) collective-permute-start(bf16[64,4,8,1]{3,0,2,1:T(8,128)(2,1)S(1)} %get-tuple-element.129), channel_id=1, source_target_pairs={{0,16},{16,32},{32,48},{48,64},{64,80},{80,96},{96,112},{1,17},{17... | collective-permute-start | bytes 12296 | tf_op jit(solution)/shard_map/ppermute | solution.py:17
  205.8 1.3 collective-permute-start.15
  207.4 3.9 collective-permute-done.15
  211.9 1.1 fusion.602
  221.6 1.0 convolution_bitcast_fusion.24
  222.8 1.0 convolution_bitcast_fusion.20
  223.9 1.0 convolution_bitcast_fusion.21
  225.1 1.0 convolution_bitcast_fusion.22
  226.3 1.0 convolution_bitcast_fusion.26
  227.4 1.0 convolution_bitcast_fusion.27
  228.6 1.0 convolution_bitcast_fusion.28
  229.8 1.0 convolution_bitcast_fusion.29
  232.5 1.4 fusion.121
  235.7 71.8 %all-reduce.11.cloned.1.call-done = (f32[27,64,64]{2,1,0:T(8,128)}, f32[27,64,64]{2,1,0:T(8,128)}, f32[8,64,64]{2,1,0:T(8,128)}) async-done(((f32[27,64,64]{2,1,0:T(8,128)}, f32[27,64,64]{2,1,0:T(8,128)}, f32[8,64,64]{2,1,0:T(8,128)}), (f32[27,64,64]{2,1,0:T(8,128)}, f32[27,64,64]{2,1,0:T(8,128)}, f32[8,64,64]{2,1,0:T(8,128)})) %all-reduce.11.cloned.1.call-update) | async-done | bytes 1015824 | tf_op jit(solution)/shard_map/psum | solution.py:129
  308.5 1.0 reshape.687
  309.5 8.4 %all-to-all-start.2 = ((bf16[128,2,512]{2,1,0:T(2,128)(2,1)}), bf16[128,2,512]{2,1,0:T(2,128)(2,1)S(1)}, u32[]{:S(2)}, u32[]{:S(2)}) async-start(bf16[128,2,512]{2,1,0:T(2,128)(2,1)} %reshape.687), calls=%async_computation.2 | async-start | bytes 524288 | tf_op jit(solution)/shard_map/all_to_all | solution.py:127
  318.9 9.8 %all-to-all-done.2 = bf16[128,2,512]{2,1,0:T(2,128)(2,1)S(1)} async-done(((bf16[128,2,512]{2,1,0:T(2,128)(2,1)}), bf16[128,2,512]{2,1,0:T(2,128)(2,1)S(1)}, u32[]{:S(2)}, u32[]{:S(2)}) %all-to-all-start.2) | async-done | bytes 262176 | tf_op jit(solution)/shard_map/all_to_all | solution.py:127
  330.3 73.5 %all-reduce.9.cloned.1.call-done = (f32[27,64,64]{2,1,0:T(8,128)}, f32[27,64,64]{2,1,0:T(8,128)}, f32[8,64,64]{2,1,0:T(8,128)}) async-done(((f32[27,64,64]{2,1,0:T(8,128)}, f32[27,64,64]{2,1,0:T(8,128)}, f32[8,64,64]{2,1,0:T(8,128)}), (f32[27,64,64]{2,1,0:T(8,128)}, f32[27,64,64]{2,1,0:T(8,128)}, f32[8,64,64]{2,1,0:T(8,128)})) %all-reduce.9.cloned.1.call-update) | async-done | bytes 1015824 | tf_op jit(solution)/shard_map/psum | solution.py:129
  403.8 1.7 broadcast_multiply_fusion.2
  405.5 2.9 broadcast_multiply_fusion
  (334 shorter events, 88.2 us)
Async XLA Ops:
  7.2 39.7 %copy-start = (bf16[8,64,64]{2,1,0:T(8,128)(2,1)S(1)}, bf16[8,64,64]{2,1,0:T(8,128)(2,1)}, u32[]{:S(2)}) copy-start(bf16[8,64,64]{2,1,0:T(8,128)(2,1)} %param.11) | copy-start | bytes 196612
  9.8 20.6 %all-to-all-start.1 = ((s32[1,128,16]{2,0,1:T(1,128)}), s32[1,128,16]{2,0,1:T(1,128)S(1)}, u32[]{:S(2)}, u32[]{:S(2)}) async-start(s32[1,128,16]{2,0,1:T(1,128)} %bitcast.3), calls=%async_computation.1 | async-start | bytes 131072 | tf_op jit(solution)/shard_map/all_to_all | solution.py:86
  22.9 12.1 %copy-start.6 = (s32[2,8,128]{2,1,0:T(8,128)S(1)}, s32[2,8,128]{2,1,0:T(8,128)}, u32[]{:S(2)}) copy-start(s32[2,8,128]{2,1,0:T(8,128)} %param.14) | copy-start | bytes 24580
  30.4 15.5 %all-to-all-start = ((bf16[128,2,512]{2,1,0:T(2,128)(2,1)}), bf16[128,2,512]{2,1,0:T(2,128)(2,1)S(1)}, u32[]{:S(2)}, u32[]{:S(2)}) async-start(bf16[128,2,512]{2,1,0:T(2,128)(2,1)} %reshape.685), calls=%async_computation | async-start | bytes 524288 | tf_op jit(solution)/shard_map/all_to_all | solution.py:85
  35.0 272.5 %all-reduce.11.cloned.1.call-start = ((), (), s32[]{:S(2)}) async-start(), calls=%async_computation.4 | async-start | bytes 4063232 | tf_op jit(solution)/shard_map/psum | solution.py:129
  48.6 5.4 %collective-permute-start = (bf16[64,1,8,128]{3,0,2,1:T(8,128)(2,1)S(1)}, bf16[64,1,8,128]{3,0,2,1:T(8,128)(2,1)S(1)}, u32[]{:S(2)}, u32[]{:S(2)}) collective-permute-start(bf16[64,1,8,128]{3,0,2,1:T(8,128)(2,1)S(1)} %get-tuple-element.151), channel_id=1, source_target_pairs={{0,1},{1,2},{2,3},{3,4},{4,5},{5,6},{6,7},{7,8},{8,9},{9,10},{10,1... | collective-permute-start | bytes 393224 | tf_op jit(solution)/shard_map/ppermute | solution.py:17
  51.4 6.9 %collective-permute-start.1 = (bf16[64,1,8,128]{3,0,2,1:T(8,128)(2,1)S(1)}, bf16[64,1,8,128]{3,0,2,1:T(8,128)(2,1)S(1)}, u32[]{:S(2)}, u32[]{:S(2)}) collective-permute-start(bf16[64,1,8,128]{3,0,2,1:T(8,128)(2,1)S(1)} %get-tuple-element.152), channel_id=1, source_target_pairs={{1,0},{2,1},{3,2},{4,3},{5,4},{6,5},{7,6},{8,7},{9,8},{10,9},{11,1... | collective-permute-start | bytes 393224 | tf_op jit(solution)/shard_map/ppermute | solution.py:18
  58.6 4.3 %collective-permute-start.2 = (bf16[64,4,8,1]{3,0,2,1:T(8,128)(2,1)S(1)}, bf16[64,4,8,1]{3,0,2,1:T(8,128)(2,1)S(1)}, u32[]{:S(2)}, u32[]{:S(2)}) collective-permute-start(bf16[64,4,8,1]{3,0,2,1:T(8,128)(2,1)S(1)} %get-tuple-element.135), channel_id=1, source_target_pairs={{0,16},{16,32},{32,48},{48,64},{64,80},{80,96},{96,112},{1,17},{17... | collective-permute-start | bytes 12296 | tf_op jit(solution)/shard_map/ppermute | solution.py:17
  59.9 4.6 %collective-permute-start.3 = (bf16[64,4,8,1]{3,0,2,1:T(8,128)(2,1)S(1)}, bf16[64,4,8,1]{3,0,2,1:T(8,128)(2,1)S(1)}, u32[]{:S(2)}, u32[]{:S(2)}) collective-permute-start(bf16[64,4,8,1]{3,0,2,1:T(8,128)(2,1)S(1)} %get-tuple-element.136), channel_id=1, source_target_pairs={{16,0},{32,16},{48,32},{64,48},{80,64},{96,80},{112,96},{17,1},{33... | collective-permute-start | bytes 12296 | tf_op jit(solution)/shard_map/ppermute | solution.py:18
  69.3 1.0 copy-start.1
  83.8 4.8 %collective-permute-start.4 = (bf16[64,1,8,128]{3,0,2,1:T(8,128)(2,1)S(1)}, bf16[64,1,8,128]{3,0,2,1:T(8,128)(2,1)S(1)}, u32[]{:S(2)}, u32[]{:S(2)}) collective-permute-start(bf16[64,1,8,128]{3,0,2,1:T(8,128)(2,1)S(1)} %get-tuple-element.149), channel_id=1, source_target_pairs={{0,1},{1,2},{2,3},{3,4},{4,5},{5,6},{6,7},{7,8},{8,9},{9,10},{10,1... | collective-permute-start | bytes 393224 | tf_op jit(solution)/shard_map/ppermute | solution.py:17
  86.0 6.9 %collective-permute-start.5 = (bf16[64,1,8,128]{3,0,2,1:T(8,128)(2,1)S(1)}, bf16[64,1,8,128]{3,0,2,1:T(8,128)(2,1)S(1)}, u32[]{:S(2)}, u32[]{:S(2)}) collective-permute-start(bf16[64,1,8,128]{3,0,2,1:T(8,128)(2,1)S(1)} %get-tuple-element.150), channel_id=1, source_target_pairs={{1,0},{2,1},{3,2},{4,3},{5,4},{6,5},{7,6},{8,7},{9,8},{10,9},{11,1... | collective-permute-start | bytes 393224 | tf_op jit(solution)/shard_map/ppermute | solution.py:18
  93.2 9.6 %collective-permute-start.6 = (bf16[64,4,8,1]{3,0,2,1:T(8,128)(2,1)S(1)}, bf16[64,4,8,1]{3,0,2,1:T(8,128)(2,1)S(1)}, u32[]{:S(2)}, u32[]{:S(2)}) collective-permute-start(bf16[64,4,8,1]{3,0,2,1:T(8,128)(2,1)S(1)} %get-tuple-element.133), channel_id=1, source_target_pairs={{0,16},{16,32},{32,48},{48,64},{64,80},{80,96},{96,112},{1,17},{17... | collective-permute-start | bytes 12296 | tf_op jit(solution)/shard_map/ppermute | solution.py:17
  100.9 5.5 %collective-permute-start.7 = (bf16[64,4,8,1]{3,0,2,1:T(8,128)(2,1)S(1)}, bf16[64,4,8,1]{3,0,2,1:T(8,128)(2,1)S(1)}, u32[]{:S(2)}, u32[]{:S(2)}) collective-permute-start(bf16[64,4,8,1]{3,0,2,1:T(8,128)(2,1)S(1)} %get-tuple-element.134), channel_id=1, source_target_pairs={{16,0},{32,16},{48,32},{64,48},{80,64},{96,80},{112,96},{17,1},{33... | collective-permute-start | bytes 12296 | tf_op jit(solution)/shard_map/ppermute | solution.py:18
  111.2 1.0 copy-start.2
  125.6 1.0 copy-start.5
  133.3 8.0 %collective-permute-start.8 = (bf16[64,1,8,128]{3,0,2,1:T(8,128)(2,1)S(1)}, bf16[64,1,8,128]{3,0,2,1:T(8,128)(2,1)S(1)}, u32[]{:S(2)}, u32[]{:S(2)}) collective-permute-start(bf16[64,1,8,128]{3,0,2,1:T(8,128)(2,1)S(1)} %get-tuple-element.147), channel_id=1, source_target_pairs={{0,1},{1,2},{2,3},{3,4},{4,5},{5,6},{6,7},{7,8},{8,9},{9,10},{10,1... | collective-permute-start | bytes 393224 | tf_op jit(solution)/shard_map/ppermute | solution.py:17
  138.8 6.9 %collective-permute-start.9 = (bf16[64,1,8,128]{3,0,2,1:T(8,128)(2,1)S(1)}, bf16[64,1,8,128]{3,0,2,1:T(8,128)(2,1)S(1)}, u32[]{:S(2)}, u32[]{:S(2)}) collective-permute-start(bf16[64,1,8,128]{3,0,2,1:T(8,128)(2,1)S(1)} %get-tuple-element.148), channel_id=1, source_target_pairs={{1,0},{2,1},{3,2},{4,3},{5,4},{6,5},{7,6},{8,7},{9,8},{10,9},{11,1... | collective-permute-start | bytes 393224 | tf_op jit(solution)/shard_map/ppermute | solution.py:18
  146.0 9.5 %collective-permute-start.10 = (bf16[64,4,8,1]{3,0,2,1:T(8,128)(2,1)S(1)}, bf16[64,4,8,1]{3,0,2,1:T(8,128)(2,1)S(1)}, u32[]{:S(2)}, u32[]{:S(2)}) collective-permute-start(bf16[64,4,8,1]{3,0,2,1:T(8,128)(2,1)S(1)} %get-tuple-element.131), channel_id=1, source_target_pairs={{0,16},{16,32},{32,48},{48,64},{64,80},{80,96},{96,112},{1,17},{17... | collective-permute-start | bytes 12296 | tf_op jit(solution)/shard_map/ppermute | solution.py:17
  153.7 5.2 %collective-permute-start.11 = (bf16[64,4,8,1]{3,0,2,1:T(8,128)(2,1)S(1)}, bf16[64,4,8,1]{3,0,2,1:T(8,128)(2,1)S(1)}, u32[]{:S(2)}, u32[]{:S(2)}) collective-permute-start(bf16[64,4,8,1]{3,0,2,1:T(8,128)(2,1)S(1)} %get-tuple-element.132), channel_id=1, source_target_pairs={{16,0},{32,16},{48,32},{64,48},{80,64},{96,80},{112,96},{17,1},{33... | collective-permute-start | bytes 12296 | tf_op jit(solution)/shard_map/ppermute | solution.py:18
  155.3 0.9 copy-start.3
  187.1 6.3 %collective-permute-start.12 = (bf16[64,1,8,128]{3,0,2,1:T(8,128)(2,1)S(1)}, bf16[64,1,8,128]{3,0,2,1:T(8,128)(2,1)S(1)}, u32[]{:S(2)}, u32[]{:S(2)}) collective-permute-start(bf16[64,1,8,128]{3,0,2,1:T(8,128)(2,1)S(1)} %get-tuple-element.145), channel_id=1, source_target_pairs={{0,1},{1,2},{2,3},{3,4},{4,5},{5,6},{6,7},{7,8},{8,9},{9,10},{10,1... | collective-permute-start | bytes 393224 | tf_op jit(solution)/shard_map/ppermute | solution.py:17
  190.9 6.9 %collective-permute-start.13 = (bf16[64,1,8,128]{3,0,2,1:T(8,128)(2,1)S(1)}, bf16[64,1,8,128]{3,0,2,1:T(8,128)(2,1)S(1)}, u32[]{:S(2)}, u32[]{:S(2)}) collective-permute-start(bf16[64,1,8,128]{3,0,2,1:T(8,128)(2,1)S(1)} %get-tuple-element.146), channel_id=1, source_target_pairs={{1,0},{2,1},{3,2},{4,3},{5,4},{6,5},{7,6},{8,7},{9,8},{10,9},{11,1... | collective-permute-start | bytes 393224 | tf_op jit(solution)/shard_map/ppermute | solution.py:18
  198.0 9.3 %collective-permute-start.14 = (bf16[64,4,8,1]{3,0,2,1:T(8,128)(2,1)S(1)}, bf16[64,4,8,1]{3,0,2,1:T(8,128)(2,1)S(1)}, u32[]{:S(2)}, u32[]{:S(2)}) collective-permute-start(bf16[64,4,8,1]{3,0,2,1:T(8,128)(2,1)S(1)} %get-tuple-element.129), channel_id=1, source_target_pairs={{0,16},{16,32},{32,48},{48,64},{64,80},{80,96},{96,112},{1,17},{17... | collective-permute-start | bytes 12296 | tf_op jit(solution)/shard_map/ppermute | solution.py:17
  205.8 5.5 %collective-permute-start.15 = (bf16[64,4,8,1]{3,0,2,1:T(8,128)(2,1)S(1)}, bf16[64,4,8,1]{3,0,2,1:T(8,128)(2,1)S(1)}, u32[]{:S(2)}, u32[]{:S(2)}) collective-permute-start(bf16[64,4,8,1]{3,0,2,1:T(8,128)(2,1)S(1)} %get-tuple-element.130), channel_id=1, source_target_pairs={{16,0},{32,16},{48,32},{64,48},{80,64},{96,80},{112,96},{17,1},{33... | collective-permute-start | bytes 12296 | tf_op jit(solution)/shard_map/ppermute | solution.py:18
  207.3 3.9 copy-start.4
  235.7 168.1 %all-reduce.9.cloned.1.call-start = ((), (), s32[]{:S(2)}) async-start(), calls=%async_computation.3 | async-start | bytes 4063232 | tf_op jit(solution)/shard_map/psum | solution.py:129
  308.2 9.7 %copy-start.7 = (s32[1,128]{1,0:T(1,128)S(1)}, s32[1,128]{1,0:T(1,128)}, u32[]{:S(2)}) copy-start(s32[1,128]{1,0:T(1,128)} %param.10) | copy-start | bytes 1540
  309.5 19.2 %all-to-all-start.2 = ((bf16[128,2,512]{2,1,0:T(2,128)(2,1)}), bf16[128,2,512]{2,1,0:T(2,128)(2,1)S(1)}, u32[]{:S(2)}, u32[]{:S(2)}) async-start(bf16[128,2,512]{2,1,0:T(2,128)(2,1)} %reshape.687), calls=%async_computation.2 | async-start | bytes 524288 | tf_op jit(solution)/shard_map/all_to_all | solution.py:127
Sparse Core Ops, SparseCore 0:
  235.8 71.6 all-reduce.10
  311.3 92.5 all-reduce.8
